TPU v7x, 256 devices: a whole 4x4x8 slice. The times are simulated.
256 devices in a mesh: section: 2 (over x_lo), blk: 128 (over x_hi, y, z, core).
Axes of the slice: x: 4 (x_hi: 2, x_lo: 2; x = x_hi * 2 + x_lo), y: 4, z: 8, core: 2. Of those that a mesh axis runs over, the one named last changes fastest.
Arguments:
- raw_traces: bfloat16 [1024, 8192], P('blk', 'section'), may hold values from -6 to 6
- valid_mask: int32 [1024, 8], P('blk', 'section'), may hold values from 0 to 1, as said below
- block_order: int32 [128], replicated, may hold values from 0 to 127, each once
Outputs:
- correlations: float32 [16, 1024, 256], P('section', 'blk')
Inputs may be any that keep to these rules, and one draw needn't show every extreme that they name: `valid_mask`: a station either has no valid segment at all, or each of its segments is valid independently. `block_order`: each block index once.
All inputs are finite; a program needn't handle non-finite values.
Results may differ from a plain program's by a relative error of at most 0.0063.
Values may be sent and summed in bfloat16 or wider, within the bound.
A program may use at most 64 MiB of HBM per device.

v0:
```python
import math
import jax
import jax.numpy as jnp
from jax import lax
from jax.sharding import PartitionSpec as P

L = 1024
NF = 384
BIN_LO = 8
LAGS = 256
TAPS = 33
HW = 50
WF = 32
STEPS = 2
RIM = 66


def extended(x, sides, width):
    for axis, dim in sides:
        devices, length = (lax.axis_size(axis), x.shape[dim])
        up = [(i, (i + 1) % devices) for i in range(devices - 1)]
        down = [(j, i) for i, j in up]
        last = lax.slice_in_dim(x, length - width, length, axis=dim)
        initial = lax.slice_in_dim(x, 0, width, axis=dim)
        before = lax.ppermute(last, axis, up)
        after = lax.ppermute(initial, axis, down)
        x = jnp.concatenate([before, x, after], axis=dim)
    return x


def from_root(value, axis, source):
    kept = jnp.where(lax.axis_index(axis) == source, value, 0).astype(value.dtype)
    return lax.psum(kept, axis)


def bandpass_taps():
    offsets = jnp.arange(TAPS, dtype=jnp.float32) - (TAPS - 1) // 2
    low = BIN_LO / L
    high = (BIN_LO + NF) / L
    window = 0.5 + 0.5 * jnp.cos(2.0 * math.pi * offsets / (TAPS + 1))
    return window * (
        2.0 * high * jnp.sinc(2.0 * high * offsets) - 2.0 * low * jnp.sinc(2.0 * low * offsets)
    )


def filter_normalize(padded):
    taps = bandpass_taps()
    width = padded.shape[1] - (TAPS - 1)
    filtered = taps[0] * padded[:, 0:width]
    for offset in range(1, TAPS):
        filtered = filtered + taps[offset] * padded[:, offset : offset + width]
    magnitude = jnp.abs(filtered)
    window_sum = lax.reduce_window(
        magnitude, jnp.zeros((), magnitude.dtype), lax.add, (1, 2 * HW + 1), (1, 1), "VALID"
    )
    centre = filtered[:, HW : HW + window_sum.shape[1]]
    return (centre / (window_sum / (2 * HW + 1) + 1e-06)).astype(jnp.bfloat16)


def forward_table():
    times = jnp.arange(L, dtype=jnp.int32)[:, None]
    bins = BIN_LO + jnp.arange(NF, dtype=jnp.int32)[None, :]
    phase = jnp.mod(times * bins, L).astype(jnp.float32) * (2.0 * math.pi / L)
    return jnp.concatenate([jnp.cos(phase), -jnp.sin(phase)], axis=1).astype(jnp.bfloat16)


def lag_table():
    bins = BIN_LO + jnp.arange(NF, dtype=jnp.int32)[:, None]
    shifts = jnp.arange(LAGS, dtype=jnp.int32)[None, :] - LAGS // 2
    phase = jnp.mod(bins * shifts, L).astype(jnp.float32) * (2.0 * math.pi / L)
    scale = 1.0 / math.sqrt(NF)
    return jnp.concatenate([jnp.cos(phase) * scale, -jnp.sin(phase) * scale], axis=0)


def whiten(normalized, maskvals):
    stations = normalized.shape[0]
    framed = normalized.reshape(-1, L)
    spectra = jnp.dot(framed, forward_table(), preferred_element_type=jnp.float32)
    spectra = spectra.reshape(stations, -1, 2 * NF)
    real_part = spectra[:, :, :NF]
    imag_part = spectra[:, :, NF:]
    amplitude = jnp.sqrt(real_part * real_part + imag_part * imag_part)
    smooth = lax.reduce_window(
        amplitude,
        jnp.zeros((), amplitude.dtype),
        lax.add,
        (1, 1, 2 * WF + 1),
        (1, 1, 1),
        ((0, 0), (0, 0), (WF, WF)),
    )
    factor = maskvals[:, :, None] / (smooth / (2 * WF + 1) + 1e-06)
    return jnp.concatenate([real_part * factor, imag_part * factor], axis=2).astype(jnp.bfloat16)


def cross_lags(sources, receivers):
    source_real = sources[:, :, :NF]
    source_imag = sources[:, :, NF:]
    recv_real = receivers[:, :, :NF]
    recv_imag = receivers[:, :, NF:]
    real_sum = jnp.einsum(
        "jsf,isf->jif", source_real, recv_real, preferred_element_type=jnp.float32
    ) + jnp.einsum("jsf,isf->jif", source_imag, recv_imag, preferred_element_type=jnp.float32)
    imag_sum = jnp.einsum(
        "jsf,isf->jif", source_real, recv_imag, preferred_element_type=jnp.float32
    ) - jnp.einsum("jsf,isf->jif", source_imag, recv_real, preferred_element_type=jnp.float32)
    stacked = jnp.concatenate([real_sum, imag_sum], axis=2)
    count_src, count_rec = (stacked.shape[0], stacked.shape[1])
    lagged = jnp.dot(
        stacked.reshape(count_src * count_rec, 2 * NF), lag_table(), precision=lax.Precision.HIGHEST
    )
    return lagged.reshape(count_src, count_rec, LAGS)


def shards(raw_traces, valid_mask, block_order):
    padded = extended(raw_traces, (("section", 1),), RIM)
    normalized = filter_normalize(padded.astype(jnp.float32))
    maskvals = valid_mask.astype(jnp.float32)
    whitened = whiten(normalized, maskvals)
    mask_wire = valid_mask.astype(jnp.bfloat16)
    stations = whitened.shape[0]
    source_parts = []
    source_masks = []
    for position in range(STEPS):
        block_spec, block_mask = (
            from_root(whitened, "blk", block_order[position]),
            from_root(mask_wire, "blk", block_order[position]),
        )
        source_parts.append(block_spec)
        source_masks.append(block_mask)
    sources = jnp.concatenate(source_parts, axis=0)
    source_mask = jnp.concatenate(source_masks, axis=0).astype(jnp.float32)
    half_count = sources.shape[0] // 2
    section_index = lax.axis_index("section")
    partial_counts = jnp.dot(source_mask, maskvals.T, precision=lax.Precision.HIGHEST)
    counts = lax.psum(partial_counts, "section")
    start = jnp.int32(0)

    def one_block(offset):
        block_spec = lax.dynamic_slice_in_dim(sources, start + offset * stations, stations, 0)
        return cross_lags(block_spec, whitened)

    lagged = lax.map(
        one_block, jnp.arange(half_count * lax.axis_size("section") // stations, dtype=jnp.int32)
    )
    summed_lags = lax.psum_scatter(
        lagged.reshape(half_count * lax.axis_size("section"), stations, LAGS),
        "section",
        scatter_dimension=0,
        tiled=True,
    )
    own_counts = lax.dynamic_slice_in_dim(counts, section_index * half_count, half_count, 0)
    return summed_lags / jnp.maximum(own_counts, 1.0)[:, :, None]


def solution(mesh):
    return jax.shard_map(
        shards,
        mesh=mesh,
        in_specs=(P("blk", "section"), P("blk", "section"), P()),
        out_specs=P("section", "blk", None),
        check_vma=False,
    )
```

profile of v0, /device:TPU:1, one launch (start us, length us, event | category | flops | bytes accessed | tf_op | source)
XLA Modules:
  0.0 1282.6 jit_solution(17670595992251923281)
XLA Ops:
  6.5 0.0 all-reduce.3.cloned.1.call-start
  6.5 0.8 fusion.72
  7.4 3.9 collective-permute-start
  11.3 1.3 collective-permute-start.1
  12.6 0.1 fusion.65
  12.7 0.7 fusion.74
  13.4 6.5 cosine_convert_fusion
  19.9 0.0 copy-done.2
  19.9 0.6 fusion.73
  21.8 0.0 copy-done.1
  21.8 0.6 broadcast_select_fusion.3
  22.4 0.7 fusion.75
  23.1 0.0 collective-permute-done
  23.1 0.0 collective-permute-done.1
  23.1 0.1 concatenate.29
  23.2 21.8 %fusion.69 = (f32[8,4196]{1,0:T(8,128)S(1)}, f32[8,4196]{1,0:T(8,128)S(1)}) fusion(f32[8,4228]{1,0:T(8,128)S(1)} %convert_element_type.37, f32[]{:T(128)} %bitcast.38, f32[]{:T(128)} %bitcast.37, f32[]{:T(128)} %bitcast.36, f32[]{:T(128)} %bitcast.35, f32[]{:T(128)} %bitcast.34, f32[]{:T(128)} %bitcast.33, f32[]{:T(128)} %bitcast.32, f32[]{:T(128)} %bitcast.31, ...), kind=kLoop, calls=%fused_computation.155 | loop fusion | flops 2215488 | bytes 4699652 | tf_op jit(solution)/shard_map/abs | solution.py:52
  45.0 65.2 %reduce_window.14 = f32[8,4096]{1,0:T(8,128)S(1)} reduce-window(f32[8,4196]{1,0:T(8,128)S(1)} %get-tuple-element.93, f32[]{:T(128)} %constant.132.clone.1), window={size=1x101}, to_apply=%region_0.2 | reduce-window | flops 3276800 | bytes 265348 | tf_op jit(solution)/shard_map/reduce_window | solution.py:53
  110.2 0.1 fusion.49
  110.3 0.4 fusion.15
  110.7 12.9 %reduce_window.15 = f32[8,4,384]{2,0,1:T(8,128)S(1)} reduce-window(f32[8,4,384]{2,0,1:T(8,128)S(1)} %add_sqrt_fusion, f32[]{:T(128)} %constant.132.clone.1), window={size=1x1x65 pad=0_0x0_0x32_32}, to_apply=%region_1.3 | reduce-window | flops 786432 | bytes 98308 | tf_op jit(solution)/shard_map/reduce_window | solution.py:83
  123.6 0.1 multiply_convert_fusion.1
  123.7 0.6 pad_maximum_fusion.1
  124.3 0.0 all-reduce.3.cloned.1.call-update
  124.4 0.0 reduce-scatter.2.cloned.1.call-start
  124.5 1116.5 %all-reduce.3.cloned.1.call-done = (bf16[8,4,768]{2,0,1:T(8,128)(2,1)}, bf16[8,4,768]{2,0,1:T(8,128)(2,1)}, bf16[8,4]{0,1:T(4,128)(2,1)}, bf16[8,4]{0,1:T(4,128)(2,1)}) async-done(((bf16[8,4,768]{2,0,1:T(8,128)(2,1)}, bf16[8,4,768]{2,0,1:T(8,128)(2,1)}, bf16[8,4]{0,1:T(4,128)(2,1)}, bf16[8,4]{0,1:T(4,128)(2,1)}), (bf16[8,4,768]{2,0,1:T(8,128)(2,1)}, bf16[8,4,768]{2,0,1:T(8,128)(2,1)}, ...) | async-done | bytes 98448 | tf_op jit(solution)/shard_map/psum | solution.py:33
  1241.0 0.8 pad_maximum_fusion
  1241.8 0.0 copy-start.3
  1241.8 0.0 copy-start.4
  1241.9 19.7 %while.12 = (s32[]{:T(128)}, f32[2,8,8,256]{3,2,1,0:T(8,128)}, s32[2]{0:T(128)S(1)}, bf16[16,4,768]{2,0,1:T(8,128)(2,1)S(1)}, bf16[8,4,768]{2,1,0:T(4,128)(2,1)S...) while((s32[]{:T(128)}, f32[2,8,8,256]{3,2,1,0:T(8,128)}, s32[2]{0:T(128)S(1)}, ...), condition=%wide.region_5.7_spmd, body=%wide.region_4.6_spmd.sunk | while | flops 153748096 | bytes 4200115 | solution.py:142
  1241.9 0.6 dynamic_slice.19
  1243.1 0.2 copy.27
  1243.4 0.3 copy.28
  1243.7 0.6 fusion.114
  1244.3 0.5 copy.29
  1244.8 0.3 copy.30
  1245.1 0.3 copy.31
  1245.4 0.6 fusion.115
  1246.0 0.5 copy.32
  1246.5 0.7 fusion.116
  1247.2 0.5 copy.33
  1247.7 0.7 fusion.117
  1248.4 0.5 copy.34
  1249.0 1.6 cosine_multiply_fusion.2
  1250.6 1.1 fusion.118
  1251.7 0.6 dynamic_slice.19
  1253.0 0.2 copy.27
  1253.3 0.3 copy.28
  1253.5 0.6 fusion.114
  1254.2 0.5 copy.29
  1254.7 0.3 copy.30
  1255.0 0.3 copy.31
  1255.2 0.6 fusion.115
  1255.9 0.5 copy.32
  1256.4 0.7 fusion.116
  1257.1 0.5 copy.33
  1257.6 0.7 fusion.117
  1258.2 0.5 copy.34
  1258.8 1.6 cosine_multiply_fusion.2
  1260.4 1.2 fusion.118
  1261.6 0.0 reduce-scatter.2.cloned.1.call-update
  1261.6 0.3 fusion.50
  1261.9 3.8 psum.39
  1265.7 8.3 reduce-scatter.2.cloned.1.call-done
  1274.0 1.5 broadcast_divide_fusion
  (24 shorter events, 0.2 us)
Async XLA Ops:
  6.5 16.6 %copy-start = (bf16[8,4096]{1,0:T(8,128)(2,1)S(1)}, bf16[8,4096]{1,0:T(8,128)(2,1)}, u32[]{:S(2)}) copy-start(bf16[8,4096]{1,0:T(8,128)(2,1)} %param.6) | copy-start | bytes 196612
  6.5 13.4 %copy-start.2 = (s32[128]{0:T(128)S(1)}, s32[128]{0:T(128)}, u32[]{:S(2)}) copy-start(s32[128]{0:T(128)} %param.8) | copy-start | bytes 1540
  6.5 15.2 %copy-start.1 = (s32[8,4]{0,1:T(4,128)S(1)}, s32[8,4]{0,1:T(4,128)}, u32[]{:S(2)}) copy-start(s32[8,4]{0,1:T(4,128)} %param.7) | copy-start | bytes 388
  6.5 1234.5 %all-reduce.3.cloned.1.call-start = ((), (), s32[]{:S(2)}) async-start(), calls=%async_computation.2 | async-start | bytes 200704 | tf_op jit(solution)/shard_map/psum | solution.py:33
  7.4 15.7 %collective-permute-start = (bf16[8,66]{1,0:T(8,128)(2,1)S(1)}, bf16[8,66]{1,0:T(8,128)(2,1)S(1)}, u32[]{:S(2)}, u32[]{:S(2)}) collective-permute-start(bf16[8,66]{1,0:T(8,128)(2,1)S(1)} %get-tuple-element.106), channel_id=1, source_target_pairs={{0,128},{1,129},{2,130},{3,131},{4,132},{5,133},{6,134},{7,135},{8... | collective-permute-start | bytes 3176 | tf_op jit(solution)/shard_map/ppermute | solution.py:25
  11.3 11.8 collective-permute-start.1
  124.4 1149.7 %reduce-scatter.2.cloned.1.call-start = ((), (), s32[]{:S(2)}) async-start(), calls=%async_computation.1 | async-start | bytes 196608 | tf_op jit(solution)/shard_map/reduce_scatter | solution.py:145
  1241.8 19.8 %copy-start.3 = (bf16[8,4]{0,1:T(4,128)(2,1)S(1)}, bf16[8,4]{0,1:T(4,128)(2,1)}, u32[]{:S(2)}) copy-start(bf16[8,4]{0,1:T(4,128)(2,1)} %get-tuple-element.91) | copy-start | bytes 196
  1241.8 19.8 %copy-start.4 = (bf16[8,4]{0,1:T(4,128)(2,1)S(1)}, bf16[8,4]{0,1:T(4,128)(2,1)}, u32[]{:S(2)}) copy-start(bf16[8,4]{0,1:T(4,128)(2,1)} %get-tuple-element.92) | copy-start | bytes 196
Sparse Core Ops, SparseCore 0:
  124.5 1116.4 all-reduce.2
  1261.7 12.2 reduce-scatter.1
where the time goes:
time: 1290 us; the launch traced here: 1280 us
  waiting for transfers between devices  1120 us (87%)
  other arithmetic  114 us (9%)
  between operations  15.1 us (1%)
    psum x1, waiting for transfers between devices, from_root(): return lax.psum(kept, axis)  1120 us
    another operation x1, other arithmetic, filter_normalize(): lax.reduce_window(magnitude, jnp.zeros((), magnitude.dtype), lax.add, (1,...  65.2 us
  transfers between devices with their start and end apart: 4, of which 2 were waited for; matrix products, arithmetic and copies ran while one was open for 1% of the time, Pallas kernels for 0%

commit v1 on v0

--- a/solution.py
+++ b/solution.py
@@ -30,7 +30,7 @@
 
 def from_root(value, axis, source):
     kept = jnp.where(lax.axis_index(axis) == source, value, 0).astype(value.dtype)
-    return lax.psum(kept, axis)
+    return jnp.sum(lax.all_gather(kept, axis), axis=0)
 
 
 def bandpass_taps():

time: 1290 us -> 534 us (0.41)
  waiting for transfers between devices: 1120 us -> 5.77 us
  blocking collectives: 3.83 us -> 366 us
    psum x1 -> x0, waiting for transfers between devices: 1120 us -> none  [from_root(): return lax.psum(kept, axis)]
    all_gather x0 -> x2, blocking collectives: none -> 362 us  [from_root(): return jnp.sum(lax.all_gather(kept, axis), axis=0)]
  transfers between devices with their start and end apart: 4 -> 5, of which waited for: 2 -> 1; matrix products, arithmetic and copies ran while one was open for 1% -> 2% of each run, Pallas kernels for 0% -> 0%
where the time goes in v1:
time: 534 us; the launch traced here: 523 us
  blocking collectives  366 us (69%)
  other arithmetic  111 us (21%)
  between operations  15 us (3%)
  local copies, waits for them, and re-layouts  11.6 us (2%)
  matrix products  6.89 us (1%)
  waiting for transfers between devices  5.77 us (1%)
    all_gather x2, blocking collectives, from_root(): return jnp.sum(lax.all_gather(kept, axis), axis=0)  362 us
    another operation x1, other arithmetic, filter_normalize(): lax.reduce_window(magnitude, jnp.zeros((), magnitude.dtype), lax.add, (1,...  56.6 us
    abs x1, other arithmetic, filter_normalize(): magnitude = jnp.abs(filtered)  21.9 us
    another operation x1, other arithmetic, whiten(): lax.reduce_window(amplitude, jnp.zeros((), amplitude.dtype), lax.add, (1,...  12.9 us
  transfers between devices with their start and end apart: 5, of which 1 were waited for; matrix products, arithmetic and copies ran while one was open for 2% of the time, Pallas kernels for 0%

profile of v1, /device:TPU:1, one launch (start us, length us, event | category | flops | bytes accessed | tf_op | source)
XLA Modules:
  0.0 523.4 jit_solution(5941018040268232980)
XLA Ops:
  6.5 0.8 fusion.72
  7.4 3.9 collective-permute-start
  11.3 1.3 collective-permute-start.1
  12.6 0.1 fusion.65
  12.7 0.7 fusion.74
  13.4 0.7 fusion.75
  14.1 6.5 %cosine_convert_fusion = (bf16[1024,384]{1,0:T(8,128)(2,1)S(1)}, bf16[1024,384]{1,0:T(8,128)(2,1)S(1)}) fusion(s32[384]{0:T(512)S(1)} %iota_add_fusion.2), kind=kLoop, calls=%fused_computation.33 | loop fusion | flops 6684672 | bytes 1574400 | tf_op jit(solution)/shard_map/convert.10
  20.6 0.6 fusion.73
  22.5 0.1 concatenate.47
  22.6 21.9 %fusion.69 = (f32[8,4196]{1,0:T(8,128)S(1)}, f32[8,4196]{1,0:T(8,128)S(1)}) fusion(f32[8,4228]{1,0:T(8,128)S(1)} %convert_element_type.56, f32[]{:T(128)} %bitcast.38, f32[]{:T(128)} %bitcast.37, f32[]{:T(128)} %bitcast.36, f32[]{:T(128)} %bitcast.35, f32[]{:T(128)} %bitcast.34, f32[]{:T(128)} %bitcast.33, f32[]{:T(128)} %bitcast.32, f32[]{:T(128)} %bitcast.31, ...), kind=kLoop, calls=%fused_computation.156 | loop fusion | flops 2215488 | bytes 4699652 | tf_op jit(solution)/shard_map/abs | solution.py:52
  44.5 56.6 %reduce_window.14 = f32[8,4096]{1,0:T(8,128)S(1)} reduce-window(f32[8,4196]{1,0:T(8,128)S(1)} %get-tuple-element.94, f32[]{:T(128)} %constant.136.clone.1), window={size=1x101}, to_apply=%region_0.2 | reduce-window | flops 3276800 | bytes 265348 | tf_op jit(solution)/shard_map/reduce_window | solution.py:53
  101.1 0.1 fusion.49
  101.2 0.4 fusion.15
  101.6 12.9 %reduce_window.15 = f32[8,4,384]{2,0,1:T(8,128)S(1)} reduce-window(f32[8,4,384]{2,0,1:T(8,128)S(1)} %add_sqrt_fusion, f32[]{:T(128)} %constant.136.clone.1), window={size=1x1x65 pad=0_0x0_0x32_32}, to_apply=%region_1.3 | reduce-window | flops 786432 | bytes 98308 | tf_op jit(solution)/shard_map/reduce_window | solution.py:83
  114.5 0.1 multiply_convert_fusion.1
  114.5 0.7 broadcast_select_fusion.1
  115.2 0.0 all-gather.9.cloned.1.call-start
  115.3 0.7 all-gather.9.cloned.1.call-update
  116.0 0.0 reduce-scatter.2.cloned.1.call-start
  116.1 186.2 %all-gather.2 = bf16[128,8,4]{1,2,0:T(4,128)(2,1)S(1)} all-gather(bf16[1,8,4]{1,2,0:T(4,128)(2,1)S(1)} %get-tuple-element.110), channel_id=2, replica_groups=mesh['section'=2,'blk'=128] {'blk'}, dimensions={0}, use_global_device_ids=true | all-gather | bytes 8256 | tf_op jit(solution)/shard_map/all_gather | solution.py:33
  302.3 0.1 reduce_sum.50
  302.4 175.3 %all-gather.3 = bf16[128,8,4]{1,2,0:T(4,128)(2,1)S(1)} all-gather(bf16[1,8,4]{1,2,0:T(4,128)(2,1)S(1)} %get-tuple-element.111), channel_id=3, replica_groups=mesh['section'=2,'blk'=128] {'blk'}, dimensions={0}, use_global_device_ids=true | all-gather | bytes 8256 | tf_op jit(solution)/shard_map/all_gather | solution.py:33
  477.8 0.1 reduce_sum.51
  478.0 0.0 all-gather.7.cloned.1.call-done
  478.0 3.7 reduce_sum.48
  481.7 0.0 all-gather.9.cloned.1.call-done
  481.7 3.7 reduce_sum.49
  485.4 20.1 %while.12 = (s32[]{:T(128)}, f32[2,8,8,256]{3,2,1,0:T(8,128)}, s32[2]{0:T(128)S(1)}, bf16[16,4,768]{2,0,1:T(8,128)(2,1)S(1)}, bf16[8,4,768]{2,1,0:T(4,128)(2,1)S...) while((s32[]{:T(128)}, f32[2,8,8,256]{3,2,1,0:T(8,128)}, s32[2]{0:T(128)S(1)}, ...), condition=%wide.region_5.7_spmd, body=%wide.region_4.6_spmd.sunk | while | flops 153748096 | bytes 5248239 | solution.py:142
  485.7 0.6 dynamic_slice.19
  486.9 0.2 copy.28
  487.2 0.3 copy.29
  487.5 0.6 fusion.114
  488.1 0.5 copy.30
  488.7 0.3 copy.31
  488.9 0.3 copy.32
  489.2 0.6 fusion.115
  489.8 0.5 copy.33
  490.4 0.7 fusion.116
  491.0 0.5 copy.34
  491.5 0.7 fusion.117
  492.2 0.5 copy.35
  492.8 1.6 cosine_multiply_fusion.2
  494.4 0.5 fusion.118
  494.9 0.6 copy-done.1
  495.6 0.6 dynamic_slice.19
  496.9 0.2 copy.28
  497.1 0.3 copy.29
  497.4 0.6 fusion.114
  498.1 0.5 copy.30
  498.6 0.3 copy.31
  498.8 0.3 copy.32
  499.1 0.6 fusion.115
  499.8 0.5 copy.33
  500.3 0.7 fusion.116
  500.9 0.5 copy.34
  501.4 0.7 fusion.117
  502.1 0.5 copy.35
  502.7 1.6 cosine_multiply_fusion.2
  504.3 0.5 fusion.118
  504.9 0.6 copy-done.1
  505.5 0.3 fusion.50
  505.8 4.1 psum.7
  509.9 5.0 reduce-scatter.2.cloned.1.call-done
  514.9 1.5 broadcast_divide_fusion
  (38 shorter events, 0.3 us)
Async XLA Ops:
  6.5 16.0 %copy-start.2 = (bf16[8,4096]{1,0:T(8,128)(2,1)S(1)}, bf16[8,4096]{1,0:T(8,128)(2,1)}, u32[]{:S(2)}) copy-start(bf16[8,4096]{1,0:T(8,128)(2,1)} %param.6) | copy-start | bytes 196612
  6.5 14.1 %copy-start.4 = (s32[128]{0:T(128)S(1)}, s32[128]{0:T(128)}, u32[]{:S(2)}) copy-start(s32[128]{0:T(128)} %param.8) | copy-start | bytes 1540
  6.5 14.7 %copy-start.3 = (s32[8,4]{0,1:T(4,128)S(1)}, s32[8,4]{0,1:T(4,128)}, u32[]{:S(2)}) copy-start(s32[8,4]{0,1:T(4,128)} %param.7) | copy-start | bytes 388
  6.5 471.4 %all-gather.7.cloned.1.call-start = ((), (), s32[]{:S(2)}) async-start(), calls=%async_computation.1 | async-start | bytes 6340608 | tf_op jit(solution)/shard_map/all_gather | solution.py:33
  7.4 15.1 %collective-permute-start = (bf16[8,66]{1,0:T(8,128)(2,1)S(1)}, bf16[8,66]{1,0:T(8,128)(2,1)S(1)}, u32[]{:S(2)}, u32[]{:S(2)}) collective-permute-start(bf16[8,66]{1,0:T(8,128)(2,1)S(1)} %get-tuple-element.107), channel_id=1, source_target_pairs={{0,128},{1,129},{2,130},{3,131},{4,132},{5,133},{6,134},{7,135},{8... | collective-permute-start | bytes 3176 | tf_op jit(solution)/shard_map/ppermute | solution.py:25
  11.3 11.2 %collective-permute-start.1 = (bf16[8,66]{1,0:T(8,128)(2,1)S(1)}, bf16[8,66]{1,0:T(8,128)(2,1)S(1)}, u32[]{:S(2)}, u32[]{:S(2)}) collective-permute-start(bf16[8,66]{1,0:T(8,128)(2,1)S(1)} %get-tuple-element.106), channel_id=1, source_target_pairs={{128,0},{129,1},{130,2},{131,3},{132,4},{133,5},{134,6},{135,7},{1... | collective-permute-start | bytes 3176 | tf_op jit(solution)/shard_map/ppermute | solution.py:26
  115.2 366.5 %all-gather.9.cloned.1.call-start = ((), (), s32[]{:S(2)}) async-start(), calls=%async_computation.2 | async-start | bytes 6340608 | tf_op jit(solution)/shard_map/all_gather | solution.py:33
  116.0 398.9 %reduce-scatter.2.cloned.1.call-start = ((), (), s32[]{:S(2)}) async-start(), calls=%async_computation.3 | async-start | bytes 196608 | tf_op jit(solution)/shard_map/reduce_scatter | solution.py:145
  492.2 2.2 copy-start
  494.9 0.7 copy-start.1
  502.1 2.2 copy-start
  504.9 0.7 copy-start.1
Sparse Core Ops, SparseCore 0:
  115.3 128.8 all-gather.6
  248.0 120.7 all-gather.8
  505.6 9.2 reduce-scatter.1
